TPU v7x, 32 devices: a whole 2x2x4 slice. The times are simulated.
32 devices in a mesh: segment: 2 (over y), expert: 16 (over z, x, core).
Axes of the slice: x: 2, y: 2, z: 4, core: 2. Of those that a mesh axis runs over, the one named last changes fastest.
Arguments:
- hidden: bfloat16 [2, 512, 2048], P('segment', 'expert'), may hold values from -6 to 6
- memory: bfloat16 [2, 512, 2048], P('segment', 'expert'), may hold values from -6 to 6
- lengths: int32 [2, 16], P('segment', 'expert'), may hold values from 1 to 32, as said below
- memory_lengths: int32 [2, 16], P('segment', 'expert'), may hold values from 1 to 32, as said below
- routes: int32 [2, 512, 2], P('segment', 'expert'), may hold values from 0 to 3, all different within a row; in each aligned block of 32 rows (0 to 31, 32 to 63, ..., all dimensions but the last counted through in order) at most 20 rows name the same one
- norm_gain: float32 [2, 3, 2048], P('segment'), may hold values from 0.5 to 1.5, as said below
- router: bfloat16 [2, 2048, 4], P('segment'), may hold values from -0.26516504 to 0.26516504, as said below
- w_in: bfloat16 [2, 2048, 16384], P('segment', None, 'expert'), may hold values from -0.13258252 to 0.13258252, as said below
- w_out: bfloat16 [2, 16384, 2048], P('segment', 'expert'), may hold values from -0.125 to 0.125, as said below
- shortlist: bfloat16 [2, 2048, 512], P('segment'), may hold values from -0.375 to 0.375
- student: float32 [2, 512, 512], P('segment', 'expert'), may hold values from -15 to 15
- targets: int32 [2, 512], P('segment', 'expert'), may hold values from 0 to 511
Outputs:
- layer_out: bfloat16 [2, 512, 2048], P('segment', 'expert')
- loss: float32 [], replicated
Inputs may be any that keep to these rules, and one draw needn't show every extreme that they name: `lengths`: every sequence has at least one position; the first sequence of each section has 32. `memory_lengths`: every sequence has at least one position; the first sequence of each section has 32. `routes`: A token's two experts differ. In the 32 rows of one device no expert is named more than 20 times, a bound that some block reaches. `norm_gain`: equal in all encoder sections, and equal in all decoder sections. `router`: equal in all encoder sections, and equal in all decoder sections. `w_in`: equal in all encoder sections, and equal in all decoder sections. `w_out`: equal in all encoder sections, and equal in all decoder sections.
All inputs are finite; a program needn't handle non-finite values.
Results may differ from a plain program's by a relative error of at most 0.0049.
Values may be sent and summed in bfloat16 or wider, within the bound.
A program may use at most 64 MiB of HBM per device.

v0:
```python
import math

import jax
import jax.numpy as jnp
from jax import lax
from jax.sharding import PartitionSpec as P

HEADS = 16
HEAD_DIM = 128
LEN = 32


epsilon = 1e-05


def passed_along(block, axis, distance):
    devices = range(lax.axis_size(axis))
    route = [(i - distance, i) for i in devices if i - distance in devices]
    return lax.ppermute(block, axis, route)


def layer_norm(values, gain_row):
    centred = values - jnp.mean(values, axis=-1, keepdims=True)
    spread = jnp.mean(centred * centred, axis=-1, keepdims=True)
    return centred * lax.rsqrt(spread + epsilon) * gain_row


def expert_rows(received, first_weight, second_weight):
    sources = received.shape[0]
    slot_count = received.shape[1]
    model_width = received.shape[2]
    flat_rows = received.reshape(sources * slot_count, model_width)
    activated = jnp.maximum(
        jnp.dot(flat_rows, first_weight, preferred_element_type=jnp.float32), 0.0
    ).astype(jnp.bfloat16)
    partial_out = jnp.dot(activated, second_weight, preferred_element_type=jnp.float32).astype(
        jnp.bfloat16
    )
    return partial_out.reshape(sources, slot_count, model_width)


def local(
    hidden,
    memory,
    lengths,
    memory_lengths,
    routes,
    norm_gain,
    router,
    w_in,
    w_out,
    shortlist,
    student,
    targets,
):
    segment_index = lax.axis_index("segment")
    half_segments = lax.axis_size("segment") // 2
    expert_count = lax.axis_size("expert")
    experts = router.shape[2]
    group_size = expert_count // experts
    tok_rows = hidden.shape[1]
    model_width = hidden.shape[2]
    capacity = 5 * tok_rows // 8
    decoder = segment_index >= half_segments
    positions = jnp.arange(tok_rows) % LEN
    seq_index = jnp.arange(tok_rows) // LEN
    is_valid = positions < lengths[0][seq_index]
    key_mask = (positions < memory_lengths[0][seq_index]).astype(jnp.bfloat16)
    arrived, arrived_mask = passed_along((memory[0], key_mask), "segment", half_segments)
    states = hidden[0].astype(jnp.float32)
    gain_rows = norm_gain[0]
    seq_count = tok_rows // LEN
    score_scale = 1.0 / math.sqrt(HEAD_DIM)
    queries = (
        layer_norm(states, gain_rows[0])
        .astype(jnp.bfloat16)
        .reshape(seq_count, LEN, HEADS, HEAD_DIM)
    )
    key_rows = arrived.reshape(seq_count, LEN, HEADS, HEAD_DIM)
    scores = (
        jnp.einsum("bqhd,bkhd->bhqk", queries, key_rows, preferred_element_type=jnp.float32)
        * score_scale
    )
    allowed = arrived_mask.reshape(seq_count, 1, 1, LEN) > 0.5
    scores = jnp.where(allowed, scores, -1e30)
    weights = jax.nn.softmax(scores, axis=-1).astype(jnp.bfloat16)
    attended = jnp.einsum(
        "bhqk,bkhd->bqhd", weights, key_rows, preferred_element_type=jnp.float32
    ).reshape(tok_rows, model_width)
    mid_states = states + jnp.where(decoder, attended, 0.0)
    normed = layer_norm(mid_states, gain_rows[1]).astype(jnp.bfloat16)
    router_probs = jax.nn.softmax(
        jnp.dot(normed, router[0], preferred_element_type=jnp.float32), axis=-1
    )
    expert_ids = jnp.arange(experts)
    first_hot = (routes[0][:, 0:1] == expert_ids).astype(jnp.float32)
    second = (routes[0][:, 1:2] == expert_ids).astype(jnp.float32)
    prob_first = jnp.sum(router_probs * first_hot, axis=-1, keepdims=True)
    prob_second = jnp.sum(router_probs * second, axis=-1, keepdims=True)
    prob_total = prob_first + prob_second
    gate_rows = (prob_first * first_hot + prob_second * second) / prob_total
    chosen = (first_hot + second) * is_valid[:, None].astype(jnp.float32)
    slot_rank = jnp.cumsum(chosen, axis=0) - 1.0
    slot_ids = jnp.arange(capacity).astype(jnp.float32)
    placing = chosen.T[:, None, :] * (slot_rank.T[:, None, :] == slot_ids[None, :, None]).astype(
        jnp.float32
    )
    buffer = jnp.einsum(
        "ect,td->ecd", placing.astype(jnp.bfloat16), normed, preferred_element_type=jnp.float32
    ).astype(jnp.bfloat16)
    outgoing = jnp.broadcast_to(
        buffer[:, None], (experts, group_size, capacity, model_width)
    ).reshape(expert_count, capacity, model_width)
    partial_out = expert_rows(
        lax.all_to_all(outgoing, "expert", split_axis=0, concat_axis=0, tiled=True),
        w_in[0],
        w_out[0],
    )
    returned = lax.all_to_all(partial_out, "expert", split_axis=0, concat_axis=0, tiled=True)
    summed = (
        returned.reshape(experts, group_size, capacity, model_width).astype(jnp.float32).sum(axis=1)
    )
    weighting = placing * gate_rows.T[:, None, :]
    moe_out = jnp.einsum("ect,ecd->td", weighting, summed, precision=lax.Precision.HIGHEST)
    layer_out = (mid_states + moe_out).astype(jnp.bfloat16)
    final_normed = layer_norm(layer_out.astype(jnp.float32), gain_rows[2]).astype(jnp.bfloat16)
    teacher = jax.nn.log_softmax(
        jnp.dot(final_normed, shortlist[0], preferred_element_type=jnp.float32), axis=-1
    )
    learner = jax.nn.log_softmax(student[0], axis=-1)
    picked = (targets[0][:, None] == jnp.arange(student.shape[2])).astype(jnp.float32)
    token_loss = jnp.sum(jnp.exp(teacher) * (teacher - learner), axis=-1) - jnp.sum(
        picked * learner, axis=-1
    )
    counted = jnp.where(decoder, is_valid.astype(jnp.float32), 0.0)
    loss_sum, loss_count = lax.psum(
        (jnp.sum(token_loss * counted), jnp.sum(counted)), ("segment", "expert")
    )
    return (layer_out[None], loss_sum / loss_count)


def solution(mesh):
    placed = (
        P("segment", "expert", None),
        P("segment", "expert", None),
        P("segment", "expert"),
        P("segment", "expert"),
        P("segment", "expert", None),
        P("segment", None, None),
        P("segment", None, None),
        P("segment", None, "expert"),
        P("segment", "expert", None),
        P("segment", None, None),
        P("segment", "expert", None),
        P("segment", "expert"),
    )
    return jax.shard_map(
        local,
        mesh=mesh,
        in_specs=placed,
        out_specs=(P("segment", "expert", None), P()),
        check_vma=False,
    )
```

profile of v0, /device:TPU:0, one launch (start us, length us, event | category | flops | bytes accessed | tf_op | source)
XLA Modules:
  0.0 160.1 jit_solution(15478402184536814028)
XLA Ops:
  0.6 5.0 %collective-permute-start.1 = (bf16[32,2048]{1,0:T(8,128)(2,1)}, bf16[32,2048]{1,0:T(8,128)(2,1)S(1)}, u32[]{:S(2)}, u32[]{:S(2)}) collective-permute-start(bf16[32,2048]{1,0:T(8,128)(2,1)} %bitcast.147), channel_id=1, source_target_pairs={{0,16},{1,17},{2,18},{3,19},{4,20},{5,21},{6,22},{7,23},{8,24},{9,... | collective-permute-start | bytes 393224 | tf_op jit(solution)/shard_map/ppermute | solution.py:19
  6.3 1.3 collective-permute-start
  7.6 1.0 convert_reduce_fusion.1
  8.7 1.0 convert_bitcast_fusion
  9.7 0.7 fusion.83
  10.4 1.1 fusion.31
  11.6 0.8 slice_bitcast_fusion.1
  13.1 0.3 fusion.84
  13.4 0.2 fusion.19
  14.2 0.2 multiply_reduce_fusion
  14.4 0.3 fusion.85
  15.0 0.3 convolution_convert_fusion
  15.5 41.7 %all_to_all.10 = bf16[16,20,2048]{2,1,0:T(8,128)(2,1)} all-to-all(bf16[16,20,2048]{2,1,0:T(8,128)(2,1)S(1)} %bitcast.137), channel_id=1, replica_groups=mesh['segment'=2,'expert'=16] {'expert'}, dimensions={0} | all-to-all | bytes 2621440 | tf_op jit(solution)/shard_map/all_to_all | solution.py:115
  57.3 3.3 %reshape.327 = bf16[320,2048]{1,0:T(8,128)(2,1)} reshape(bf16[16,20,2048]{2,1,0:T(8,128)(2,1)} %all_to_all.10) | data formatting | bytes 2621440 | tf_op jit(solution)/shard_map/reshape | solution.py:32
  60.6 7.8 %fusion.5 = bf16[320,2048]{1,0:T(8,128)(2,1)} fusion(bf16[1,1024,2048]{2,1,0:T(8,128)(2,1)} %param.21, bf16[320,2048]{1,0:T(8,128)(2,1)} %reshape.327, bf16[1,2048,1024]{2,1,0:T(8,128)(2,1)} %param.20), kind=kOutput, calls=%fused_computation.6 | convolution fusion | flops 2685665280 | bytes 11010048 | tf_op jit(solution)/shard_map/dot_general | solution.py:36
  68.4 3.2 %reshape.328 = bf16[16,20,2048]{2,1,0:T(8,128)(2,1)} reshape(bf16[320,2048]{1,0:T(8,128)(2,1)} %fusion.5) | data formatting | bytes 2621440 | tf_op jit(solution)/shard_map/reshape | solution.py:39
  71.6 5.2 %all-to-all-start.1 = ((bf16[16,20,2048]{2,1,0:T(8,128)(2,1)}), bf16[16,20,2048]{2,1,0:T(8,128)(2,1)}, u32[]{:S(2)}, u32[]{:S(2)}) async-start(bf16[16,20,2048]{2,1,0:T(8,128)(2,1)} %reshape.328), calls=%async_computation.1 | async-start | bytes 3145728 | tf_op jit(solution)/shard_map/all_to_all | solution.py:119
  77.1 31.6 %all-to-all-done.1 = bf16[16,20,2048]{2,1,0:T(8,128)(2,1)} async-done(((bf16[16,20,2048]{2,1,0:T(8,128)(2,1)}), bf16[16,20,2048]{2,1,0:T(8,128)(2,1)}, u32[]{:S(2)}, u32[]{:S(2)}) %all-to-all-start.1) | async-done | bytes 1310752 | tf_op jit(solution)/shard_map/all_to_all | solution.py:119
  108.7 1.8 %convert_reduce_fusion = f32[4,20,2048]{2,1,0:T(8,128)S(1)} fusion(bf16[16,20,2048]{2,1,0:T(8,128)(2,1)} %all-to-all-done.1), kind=kLoop, calls=%fused_computation.5 | loop fusion | flops 1146880 | bytes 1966080 | tf_op jit(solution)/shard_map/reduce_sum | solution.py:121
  110.5 0.7 convert_reduce_fusion.2
  111.3 0.2 fusion.27
  111.5 0.6 fusion.86
  112.5 0.7 multiply_reduce_fusion.2
  113.2 44.5 %all-reduce = (f32[]{:T(128)}, f32[]{:T(128)}) all-reduce(f32[]{:T(128)} %get-tuple-element.25, f32[]{:T(128)} %get-tuple-element.26), channel_id=1, replica_groups=mesh['segment'=2,'expert'=16] {'segment','expert'}, use_global_device_ids=true, to_apply=%region_19.21 | all-reduce | flops 2 | bytes 16 | tf_op jit(solution)/shard_map/psum | solution.py:136
  (43 shorter events, 1.9 us)
Async XLA Ops:
  0.6 110.9 %copy-start = (bf16[1,2048,512]{2,1,0:T(8,128)(2,1)S(1)}, bf16[1,2048,512]{2,1,0:T(8,128)(2,1)}, u32[]{:S(2)}) copy-start(bf16[1,2048,512]{2,1,0:T(8,128)(2,1)} %param.22) | copy-start | bytes 6291460
  0.6 12.4 %collective-permute-start.1 = (bf16[32,2048]{1,0:T(8,128)(2,1)}, bf16[32,2048]{1,0:T(8,128)(2,1)S(1)}, u32[]{:S(2)}, u32[]{:S(2)}) collective-permute-start(bf16[32,2048]{1,0:T(8,128)(2,1)} %bitcast.147), channel_id=1, source_target_pairs={{0,16},{1,17},{2,18},{3,19},{4,20},{5,21},{6,22},{7,23},{8,24},{9,... | collective-permute-start | bytes 393224 | tf_op jit(solution)/shard_map/ppermute | solution.py:19
  6.3 6.7 %collective-permute-start = (bf16[32]{0:T(256)(128)(2,1)S(1)}, bf16[32]{0:T(256)(128)(2,1)S(1)}, u32[]{:S(2)}, u32[]{:S(2)}) collective-permute-start(bf16[32]{0:T(256)(128)(2,1)S(1)} %compare_convert_fusion.1), channel_id=1, source_target_pairs={{0,16},{1,17},{2,18},{3,19},{4,20},{5,21},{6,22},{7,23},{8,24},{9,... | collective-permute-start | bytes 200 | tf_op jit(solution)/shard_map/ppermute | solution.py:19
  8.7 5.3 %copy-start.1 = (bf16[1,32,2048]{2,1,0:T(8,128)(2,1)S(1)}, bf16[1,32,2048]{2,1,0:T(8,128)(2,1)}, u32[]{:S(2)}) copy-start(bf16[1,32,2048]{2,1,0:T(8,128)(2,1)} %param.13) | copy-start | bytes 393220
  11.6 2.8 %copy-start.5 = (bf16[1,2048,4]{1,2,0:T(4,128)(2,1)S(1)}, bf16[1,2048,4]{1,2,0:T(4,128)(2,1)}, u32[]{:S(2)}) copy-start(bf16[1,2048,4]{1,2,0:T(4,128)(2,1)} %param.19) | copy-start | bytes 49156
  71.6 5.3 %copy-start.3 = (f32[1,32,512]{2,1,0:T(8,128)S(1)}, f32[1,32,512]{2,1,0:T(8,128)}, u32[]{:S(2)}) copy-start(f32[1,32,512]{2,1,0:T(8,128)} %param.23) | copy-start | bytes 196612
  71.6 37.2 %all-to-all-start.1 = ((bf16[16,20,2048]{2,1,0:T(8,128)(2,1)}), bf16[16,20,2048]{2,1,0:T(8,128)(2,1)}, u32[]{:S(2)}, u32[]{:S(2)}) async-start(bf16[16,20,2048]{2,1,0:T(8,128)(2,1)} %reshape.328), calls=%async_computation.1 | async-start | bytes 3145728 | tf_op jit(solution)/shard_map/all_to_all | solution.py:119
  110.5 1.8 %copy-start.4 = (s32[1,32]{1,0:T(1,128)S(1)}, s32[1,32]{1,0:T(1,128)}, u32[]{:S(2)}) copy-start(s32[1,32]{1,0:T(1,128)} %param.24) | copy-start | bytes 388
  111.2 47.8 %copy-start.2 = (bf16[32,2048]{1,0:T(8,128)(2,1)}, bf16[32,2048]{1,0:T(8,128)(2,1)S(1)}, u32[]{:S(2)}) copy-start(bf16[32,2048]{1,0:T(8,128)(2,1)S(1)} %get-tuple-element.22) | copy-start | bytes 393220
where the time goes:
time: 161 us; the launch traced here: 160 us
  blocking collectives  86.2 us (54%)
  waiting for transfers between devices  31.6 us (20%)
  starting transfers between devices  11.6 us (7%)
  matrix products  10.3 us (6%)
  local copies, waits for them, and re-layouts  8.76 us (5%)
  other arithmetic  7.12 us (4%)
  between operations  4.64 us (3%)
    psum x1, blocking collectives, local(): lax.psum((jnp.sum(token_loss * counted), jnp.sum(counted)), ('segment', '...  44.5 us
    all_to_all x1, blocking collectives, local(): lax.all_to_all(outgoing, 'expert', split_axis=0, concat_axis=0, tiled=True)  41.7 us
    all_to_all x1, waiting for transfers between devices, local(): lax.all_to_all(partial_out, 'expert', split_axis=0, concat_axis=0, tiled=...  31.6 us
    dot_general x1, matrix products, expert_rows(): jnp.dot(activated, second_weight, preferred_element_type=jnp.float32)  7.8 us
    ppermute x2, starting transfers between devices, passed_along(): return lax.ppermute(block, axis, route)  6.33 us
    all_to_all x1, starting transfers between devices, local(): lax.all_to_all(partial_out, 'expert', split_axis=0, concat_axis=0, tiled=...  5.24 us
    reshape x1, local copies, waits for them, and re-layouts, expert_rows(): flat_rows = received.reshape(sources * slot_count, model_width)  3.29 us
  transfers between devices with their start and end apart: 3, of which 1 were waited for; matrix products, arithmetic and copies ran while one was open for 3% of the time, Pallas kernels for 0%

commit v1 on v0

v1 whole, which is shorter than its diff:
```python
import functools
import math

import jax
import jax.numpy as jnp
from jax import lax
from jax.experimental import pallas as pl
from jax.experimental.pallas import tpu as pltpu
from jax.sharding import PartitionSpec as P

HEAD_DIM = 128
LEN = 32
EPS = 1e-05
MESH = pl.DeviceIdType.MESH
BF = jnp.bfloat16
F32 = jnp.float32


def layer_norm(values, gain_row):
    centred = values - jnp.mean(values, axis=-1, keepdims=True)
    spread = jnp.mean(centred * centred, axis=-1, keepdims=True)
    return centred * lax.rsqrt(spread + EPS) * gain_row


def xor(a, k, count):
    out = 0
    bit = 1
    while bit < count:
        out = out + lax.rem(a // bit + (k // bit) % 2, 2) * bit
        bit *= 2
    return out


def kernel(
    n_seg, n_exp, experts, gx, gc,
    hidden, memory, lengths, memory_lengths, routes, norm_gain, router,
    w_in, w_out, shortlist, student, targets,
    layer_out, loss_out,
    win, wout, short, kmem, klen_src, klen, mid,
    out_a, out_b, x, x_b, stage, act, y0,
    core_a, core_b, rc_a, rc_b, xs_a, xs_b, rx_a, rx_b, zs_a, zs_b, z_a, z_b, z_all, z_stage,
    lsend, lrecv, gsend, grecv,
    wsem, msem, ra, rb, sz, sx, sc, rc_s, rc_r, rx_s, rx_r, rz_s, rz_r, l_s, l_r, g_s, g_r,
):
    seg = lax.axis_index("segment")
    me = lax.axis_index("expert")
    half_seg = n_seg // 2
    group = gx * gc
    e = me // group
    j = lax.rem(me, group)
    xi = j // gc
    ci = lax.rem(j, gc)
    tok = hidden.shape[1]
    width = hidden.shape[2]
    heads = width // HEAD_DIM
    cap = 5 * tok // 8
    main = cap // 16 * 16
    rest = cap - main
    hop_order = [k for k in range(experts // 2, experts)] + [k for k in range(1, experts // 2)]

    def dev(e2, x2, c2):
        return (seg, (e2 * gx + x2) * gc + c2)

    loads = [
        pltpu.make_async_copy(w_in.at[0], win, wsem.at[0]),
        pltpu.make_async_copy(w_out.at[0], wout, wsem.at[1]),
        pltpu.make_async_copy(shortlist.at[0], short, wsem.at[2]),
    ]
    for load in loads:
        load.start()

    barrier = pltpu.get_barrier_semaphore()
    for d in range(1, n_exp):
        pl.semaphore_signal(
            barrier, inc=1, device_id=(seg, lax.rem(me + d, n_exp)), device_id_type=MESH
        )
    for d in range(1, n_seg):
        pl.semaphore_signal(
            barrier, inc=1, device_id=(lax.rem(seg + d, n_seg), me), device_id_type=MESH
        )
    klen_src[...] = jnp.broadcast_to(memory_lengths[0:1, 0:1], klen_src.shape)
    for q in range(1, tok // LEN):
        klen_src[q : q + 1, :] = jnp.broadcast_to(memory_lengths[0:1, q : q + 1], (1, 128))
    gains = norm_gain[0]
    states = hidden[0].astype(F32)
    pl.semaphore_wait(barrier, n_exp - 1 + n_seg - 1)

    is_decoder = seg >= half_seg
    to_seg = lax.rem(seg + half_seg, n_seg)
    mem_copy = pltpu.make_async_remote_copy(
        memory.at[0], kmem, msem.at[0], msem.at[1], device_id=(to_seg, me), device_id_type=MESH
    )
    len_copy = pltpu.make_async_remote_copy(
        klen_src, klen, msem.at[2], msem.at[3], device_id=(to_seg, me), device_id_type=MESH
    )

    @pl.when(seg < half_seg)
    def _():
        mem_copy.start()
        len_copy.start()
        mid[...] = states

    @pl.when(seg >= half_seg)
    def _():
        queries = layer_norm(states, gains[0:1]).astype(BF)
        len_copy.wait_recv()
        mem_copy.wait_recv()
        keys = kmem[...]
        col = lax.broadcasted_iota(jnp.int32, (tok, tok), 1)
        row = lax.broadcasted_iota(jnp.int32, (tok, tok), 0)
        klen_v = klen[...]
        allowed = jnp.zeros((tok, tok), jnp.bool_)
        for q in range(tok // LEN):
            inside = (col >= q * LEN) & (col - q * LEN < klen_v[q : q + 1, 0:1])
            inside = inside & (col < (q + 1) * LEN) & (row >= q * LEN) & (row < (q + 1) * LEN)
            allowed = allowed | inside
        scores = jnp.concatenate(
            [
                jnp.where(
                    allowed,
                    lax.dot_general(
                        queries[:, h * HEAD_DIM : (h + 1) * HEAD_DIM],
                        keys[:, h * HEAD_DIM : (h + 1) * HEAD_DIM],
                        (((1,), (1,)), ((), ())),
                        preferred_element_type=F32,
                    )
                    * (1.0 / math.sqrt(HEAD_DIM)),
                    -1e30,
                )
                for h in range(heads)
            ],
            axis=0,
        )
        top = jnp.max(scores, axis=-1, keepdims=True)
        raised = jnp.exp(scores - top)
        weights = (raised / jnp.sum(raised, axis=-1, keepdims=True)).astype(BF)
        for h in range(heads):
            part = slice(h * HEAD_DIM, (h + 1) * HEAD_DIM)
            mid[:, part] = states[:, part] + jnp.dot(
                weights[h * tok : (h + 1) * tok], keys[:, part], preferred_element_type=F32
            )

    normed = layer_norm(mid[...], gains[1:2]).astype(BF)

    expert_lane = lax.broadcasted_iota(jnp.int32, (tok, experts), 1)
    pos = lax.broadcasted_iota(jnp.int32, (tok, 1), 0)
    valid = jnp.zeros((tok, 1), F32)
    for q in range(tok // LEN):
        ok = (pos >= q * LEN) & (pos < (q + 1) * LEN) & (pos - q * LEN < lengths[0:1, q : q + 1])
        valid = valid + ok.astype(F32)
    route_pair = routes[0]
    first_hot = (route_pair[:, 0:1] == expert_lane).astype(F32)
    second_hot = (route_pair[:, 1:2] == expert_lane).astype(F32)
    chosen = (first_hot + second_hot) * valid
    before = (
        lax.broadcasted_iota(jnp.int32, (tok, tok), 1)
        < lax.broadcasted_iota(jnp.int32, (tok, tok), 0)
    ).astype(BF)
    rank = jnp.dot(before, chosen.astype(BF), preferred_element_type=F32)
    n_main = experts * main
    n_slots = experts * cap
    lanes = -(-n_slots // 128) * 128
    lane = lax.broadcasted_iota(jnp.int32, (1, lanes), 1)
    slot_of = jnp.full((1, lanes), -1, jnp.int32)
    expert_of = jnp.full((1, lanes), -1, jnp.int32)
    for k in range(experts):
        ek = xor(e, k, experts)
        in_main = (lane >= k * main) & (lane < (k + 1) * main)
        low = n_main + k * rest
        in_rest = (lane >= low) & (lane < low + rest)
        slot_of = jnp.where(in_main, lane - k * main, slot_of)
        slot_of = jnp.where(in_rest, lane - low + main, slot_of)
        expert_of = jnp.where(in_main | in_rest, ek, expert_of)
    placing = jnp.zeros((tok, lanes), F32)
    for k in range(experts):
        here = (expert_of == k) & (rank[:, k : k + 1] == slot_of.astype(F32))
        placing = placing + jnp.where(here, chosen[:, k : k + 1], 0.0)
    place_rows = jnp.transpose(placing)[0:n_slots].astype(BF)
    slots = jnp.dot(place_rows, normed, preferred_element_type=F32)

    def rows_a(dc, dx, k):
        return pl.ds(dc * gx * experts * cap + (dx * experts + k) * main, main)

    def index_b(dc, dx, k):
        return (dc * gx + dx) * experts + k

    x[rows_a(0, 0, 0), :] = slots[0:main].astype(BF)
    x_b[0] = slots[n_main : n_main + rest].astype(BF)
    for k in hop_order:
        out_a[k] = slots[k * main : (k + 1) * main].astype(BF)
        out_b[k] = slots[n_main + k * rest : n_main + (k + 1) * rest].astype(BF)

    waits = []

    def send(src, dst, s_sem, r_sem, target):
        copy = pltpu.make_async_remote_copy(
            src, dst, s_sem, r_sem, device_id=target, device_id_type=MESH
        )
        copy.start()
        waits.append(copy)

    def landed(ref, sem):
        pltpu.make_async_copy(ref, ref, sem).wait()

    def forward(slot_from, slot_to, sems, base, target):
        i, o = index_b(*slot_from), index_b(*slot_to)
        send(x.at[rows_a(*slot_from)], x.at[rows_a(*slot_to)], sems.at[base], ra.at[o], target)
        send(x_b.at[i], x_b.at[o], sems.at[base + 1], rb.at[o], target)

    for k in hop_order:
        target = dev(xor(e, k, experts), xi, ci)
        o = index_b(0, 0, k)
        send(out_a.at[k], x.at[rows_a(0, 0, k)], sz.at[2 * k], ra.at[o], target)
        send(out_b.at[k], x_b.at[o], sz.at[2 * k + 1], rb.at[o], target)

    core_dev = dev(e, xi, lax.rem(ci + 1, gc))
    for k in [0] + hop_order:
        if k:
            o = index_b(0, 0, k)
            landed(x.at[rows_a(0, 0, k)], ra.at[o])
            landed(x_b.at[o], rb.at[o])
        for d in range(1, gx):
            forward(
                (0, 0, k), (0, d, k), sx, 2 * ((d - 1) * experts + k),
                dev(e, lax.rem(xi + d, gx), ci),
            )
        forward((0, 0, k), (1, 0, k), sc, 2 * k, core_dev)
    for k in [0] + hop_order:
        for d in range(1, gx):
            o = index_b(0, d, k)
            landed(x.at[rows_a(0, d, k)], ra.at[o])
            landed(x_b.at[o], rb.at[o])
            forward((0, d, k), (1, d, k), sc, 2 * (d * experts + k), core_dev)
    for k in [0] + hop_order:
        for d in range(gx):
            o = index_b(1, d, k)
            landed(x.at[rows_a(1, d, k)], ra.at[o])
            landed(x_b.at[o], rb.at[o])

    blocks = gx * experts
    half_rows = blocks * cap
    half_main = blocks * main
    for dc in range(gc):
        for i in range(blocks):
            stage[i * rest : (i + 1) * rest, :] = x_b[dc * blocks + i].astype(F32)
        x[dc * half_rows + half_main : (dc + 1) * half_rows, :] = stage[...].astype(BF)

    units = win.shape[1]
    tile = min(256, units)
    loads[0].wait()

    @pl.loop(0, units // tile)
    def _(i):
        cols = pl.ds(pl.multiple_of(i * tile, tile), tile)
        act[:, cols] = jnp.maximum(
            jnp.dot(x[...], win[:, cols], preferred_element_type=F32), 0.0
        ).astype(BF)

    loads[1].wait()
    tile2 = 256

    @pl.loop(0, width // tile2)
    def _(i):
        cols = pl.ds(pl.multiple_of(i * tile2, tile2), tile2)
        part = jnp.dot(act[half_rows:, :], wout[:, cols], preferred_element_type=F32)
        core_a[:, cols] = part[0:half_main].astype(BF)
        for b in range(blocks):
            core_b[b, :, cols] = part[half_main + b * rest : half_main + (b + 1) * rest].astype(BF)

    send(core_a, rc_a, rc_s.at[0], rc_r.at[0], core_dev)
    send(core_b, rc_b, rc_s.at[1], rc_r.at[1], core_dev)

    @pl.loop(0, width // tile2)
    def _(i):
        cols = pl.ds(pl.multiple_of(i * tile2, tile2), tile2)
        y0[:, cols] = jnp.dot(act[0:half_rows, :], wout[:, cols], preferred_element_type=F32)

    landed(rc_a, rc_r.at[0])
    landed(rc_b, rc_r.at[1])

    def chip_sum(dx, k):
        b = dx * experts + k
        sum_a = y0[b * main : (b + 1) * main, :] + rc_a[b * main : (b + 1) * main, :].astype(F32)
        low = half_main + b * rest
        sum_b = y0[low : low + rest, :] + rc_b[b].astype(F32)
        return sum_a, sum_b

    back_order = hop_order + [0]
    for k in back_order:
        for d in range(1, gx):
            o = (d - 1) * experts + k
            sum_a, sum_b = chip_sum(d, k)
            xs_a[o] = sum_a.astype(BF)
            xs_b[o] = sum_b.astype(BF)
            target = dev(e, lax.rem(xi + gx - d, gx), ci)
            send(xs_a.at[o], rx_a.at[o], rx_s.at[2 * o], rx_r.at[2 * o], target)
            send(xs_b.at[o], rx_b.at[o], rx_s.at[2 * o + 1], rx_r.at[2 * o + 1], target)
    for k in back_order:
        sum_a, sum_b = chip_sum(0, k)
        for d in range(1, gx):
            o = (d - 1) * experts + k
            landed(rx_a.at[o], rx_r.at[2 * o])
            landed(rx_b.at[o], rx_r.at[2 * o + 1])
            sum_a = sum_a + rx_a[o].astype(F32)
            sum_b = sum_b + rx_b[o].astype(F32)
        if k:
            zs_a[k] = sum_a.astype(BF)
            zs_b[k] = sum_b.astype(BF)
            target = dev(xor(e, k, experts), xi, ci)
            send(zs_a.at[k], z_a.at[k], rz_s.at[2 * k], rz_r.at[2 * k], target)
            send(zs_b.at[k], z_b.at[k], rz_s.at[2 * k + 1], rz_r.at[2 * k + 1], target)
        else:
            z_all[0:main, :] = sum_a.astype(BF)
            z_stage[0:rest, :] = sum_b

    probs = jnp.dot(normed, router[0], preferred_element_type=F32)
    probs = jnp.exp(probs - jnp.max(probs, axis=-1, keepdims=True))
    probs = probs / jnp.sum(probs, axis=-1, keepdims=True)
    prob_first = jnp.sum(probs * first_hot, axis=-1, keepdims=True)
    prob_second = jnp.sum(probs * second_hot, axis=-1, keepdims=True)
    gate = (prob_first * first_hot + prob_second * second_hot) / (prob_first + prob_second)
    combine = jnp.zeros((tok, lanes), F32)
    for k in range(experts):
        combine = combine + jnp.where(expert_of == k, gate[:, k : k + 1], 0.0)
    combine = (combine * placing)[:, 0:n_slots]
    high = combine.astype(BF)
    low = (combine - high.astype(F32)).astype(BF)

    learner_in = student[0]
    shifted = learner_in - jnp.max(learner_in, axis=-1, keepdims=True)
    learner = shifted - jnp.log(jnp.sum(jnp.exp(shifted), axis=-1, keepdims=True))
    square = lax.broadcasted_iota(jnp.int32, (tok, tok), 0) == lax.broadcasted_iota(
        jnp.int32, (tok, tok), 1
    )
    target_col = jnp.sum(
        jnp.where(square, jnp.broadcast_to(targets[0:1, :], (tok, tok)), 0).astype(F32),
        axis=-1, keepdims=True,
    )
    vocab = student.shape[2]
    picked = lax.broadcasted_iota(jnp.int32, (tok, vocab), 1).astype(F32) == target_col
    hit = jnp.sum(jnp.where(picked, learner, 0.0), axis=-1, keepdims=True)
    loads[2].wait()

    for k in hop_order:
        landed(z_a.at[k], rz_r.at[2 * k])
        landed(z_b.at[k], rz_r.at[2 * k + 1])
        z_all[k * main : (k + 1) * main, :] = z_a[k]
        z_stage[k * rest : (k + 1) * rest, :] = z_b[k].astype(F32)
    z_all[n_main:, :] = z_stage[...].astype(BF)
    back = z_all[...]
    moe = jnp.dot(high, back, preferred_element_type=F32) + jnp.dot(
        low, back, preferred_element_type=F32
    )
    out = (mid[...] + moe).astype(BF)
    layer_out[0] = out

    final = layer_norm(out.astype(F32), gains[2:3]).astype(BF)
    logits = jnp.dot(final, short[...], preferred_element_type=F32)
    logits = logits - jnp.max(logits, axis=-1, keepdims=True)
    teacher = logits - jnp.log(jnp.sum(jnp.exp(logits), axis=-1, keepdims=True))
    token_loss = jnp.sum(jnp.exp(teacher) * (teacher - learner), axis=-1, keepdims=True) - hit
    counted = jnp.where(is_decoder, valid, 0.0)
    loss_sum = jnp.sum(token_loss * counted, axis=0, keepdims=True)
    loss_count = jnp.sum(counted, axis=0, keepdims=True)
    spot = lax.broadcasted_iota(jnp.int32, lsend.shape, 1)
    pair = jnp.where(spot == 0, loss_sum, jnp.where(spot == 1, loss_count, 0.0))
    lsend[...] = pair
    lrecv[me] = pair
    for d in range(1, n_exp):
        send(
            lsend, lrecv.at[me], l_s.at[d], l_r.at[d], (seg, lax.rem(me + d, n_exp))
        )
    for d in range(1, n_exp):
        landed(lrecv.at[lax.rem(me + n_exp - d, n_exp)], l_r.at[d])
    total = lrecv[0]
    for i in range(1, n_exp):
        total = total + lrecv[i]
    gsend[...] = total
    grecv[seg] = total
    for d in range(1, n_seg):
        send(
            gsend, grecv.at[seg], g_s.at[d], g_r.at[d], (lax.rem(seg + d, n_seg), me)
        )
    for d in range(1, n_seg):
        landed(grecv.at[lax.rem(seg + n_seg - d, n_seg)], g_r.at[d])
    total = grecv[0]
    for i in range(1, n_seg):
        total = total + grecv[i]
    loss_out[...] = total[0:1, 0:1] / total[0:1, 1:2]

    for copy in waits:
        copy.wait_send()

    @pl.when(seg < half_seg)
    def _():
        mem_copy.wait_send()
        len_copy.wait_send()


def local(
    hidden, memory, lengths, memory_lengths, routes, norm_gain, router,
    w_in, w_out, shortlist, student, targets,
):
    n_seg = lax.axis_size("segment")
    n_exp = lax.axis_size("expert")
    experts = router.shape[2]
    group = n_exp // experts
    gc = 2
    gx = group // gc
    tok, width = hidden.shape[1], hidden.shape[2]
    units = w_in.shape[2]
    vocab = shortlist.shape[2]
    cap = 5 * tok // 8
    main = cap // 16 * 16
    rest = cap - main
    blocks = gx * experts
    half_rows = blocks * cap
    vm = pl.BlockSpec(memory_space=pltpu.VMEM)
    hbm = pl.BlockSpec(memory_space=pl.ANY)
    v = pltpu.VMEM
    dma = pltpu.SemaphoreType.DMA
    nx = max(gx - 1, 1) * experts
    scratch = [
        v((width, units), BF), v((units, width), BF), v((width, vocab), BF),
        v((tok, width), BF), v((8, 128), jnp.int32), v((8, 128), jnp.int32), v((tok, width), F32),
        v((experts, main, width), BF), v((experts, rest, width), BF),
        v((gc * half_rows, width), BF), v((gc * blocks, rest, width), BF),
        v((blocks * rest, width), F32), v((gc * half_rows, units), BF), v((half_rows, width), F32),
        v((blocks * main, width), BF), v((blocks, rest, width), BF),
        v((blocks * main, width), BF), v((blocks, rest, width), BF),
        v((nx, main, width), BF), v((nx, rest, width), BF),
        v((nx, main, width), BF), v((nx, rest, width), BF),
        v((experts, main, width), BF), v((experts, rest, width), BF),
        v((experts, main, width), BF), v((experts, rest, width), BF),
        v((experts * cap, width), BF), v((experts * rest, width), F32),
        v((8, 128), F32), v((n_exp, 8, 128), F32), v((8, 128), F32), v((n_seg, 8, 128), F32),
        dma((3,)), dma((4,)), dma((gc * blocks,)), dma((gc * blocks,)),
        dma((2 * experts,)), dma((2 * nx,)), dma((2 * blocks,)),
        dma((2,)), dma((2,)), dma((2 * nx,)), dma((2 * nx,)),
        dma((2 * experts,)), dma((2 * experts,)),
        dma((n_exp,)), dma((n_exp,)), dma((n_seg,)), dma((n_seg,)),
    ]
    layer_out, loss = pl.pallas_call(
        functools.partial(kernel, n_seg, n_exp, experts, gx, gc),
        out_shape=(
            jax.ShapeDtypeStruct((1, tok, width), BF),
            jax.ShapeDtypeStruct((1, 1), F32),
        ),
        in_specs=[vm, hbm, vm, vm, vm, vm, vm, hbm, hbm, hbm, vm, vm],
        out_specs=(vm, vm),
        scratch_shapes=scratch,
        compiler_params=pltpu.CompilerParams(
            collective_id=0, has_side_effects=True, vmem_limit_bytes=60 * 1024 * 1024
        ),
    )(
        hidden, memory, lengths, memory_lengths, routes, norm_gain, router,
        w_in, w_out, shortlist, student, targets,
    )
    return layer_out, loss[0, 0]


def solution(mesh):
    placed = (
        P("segment", "expert", None),
        P("segment", "expert", None),
        P("segment", "expert"),
        P("segment", "expert"),
        P("segment", "expert", None),
        P("segment", None, None),
        P("segment", None, None),
        P("segment", None, "expert"),
        P("segment", "expert", None),
        P("segment", None, None),
        P("segment", "expert", None),
        P("segment", "expert"),
    )
    return jax.shard_map(
        local,
        mesh=mesh,
        in_specs=placed,
        out_specs=(P("segment", "expert", None), P()),
        check_vma=False,
    )
```

time: 161 us -> 66.3 us (0.41)
  blocking collectives: 86.2 us -> 0 us
  Pallas kernels: 0 us -> 56.2 us
  waiting for transfers between devices: 31.6 us -> 0 us
  starting transfers between devices: 11.6 us -> 0 us
  matrix products: 10.3 us -> 0 us
  other arithmetic: 7.12 us -> 0 us
  local copies, waits for them, and re-layouts: 8.76 us -> 6.05 us
    pallas_call x0 -> x1, Pallas kernels: none -> 56.2 us  [local(): pl.pallas_call(functools.partial(kernel, n_seg, n_exp, experts, gx, gc),...]
    psum x1 -> x0, blocking collectives: 44.5 us -> none  [local(): lax.psum((jnp.sum(token_loss * counted), jnp.sum(counted)), ('segment', '...]
    all_to_all x1 -> x0, blocking collectives: 41.7 us -> none  [local(): lax.all_to_all(outgoing, 'expert', split_axis=0, concat_axis=0, tiled=True)]
    all_to_all x1 -> x0, waiting for transfers between devices: 31.6 us -> none  [local(): lax.all_to_all(partial_out, 'expert', split_axis=0, concat_axis=0, tiled=...]
    dot_general x6 -> x0, matrix products: 9.95 us -> none  [the longest x1 7.8 us: expert_rows(): jnp.dot(activated, second_weight, preferred_element_type=jnp.float32)]
    reshape x2 -> x0, local copies, waits for them, and re-layouts: 6.5 us -> none  [the longest x1 3.29 us: expert_rows(): flat_rows = received.reshape(sources * slot_count, model_width)]
    ppermute x2 -> x0, starting transfers between devices: 6.33 us -> none  [passed_along(): return lax.ppermute(block, axis, route)]
    unnamed x13 -> x4, local copies, waits for them, and re-layouts: 0.09 us -> 6.05 us
  transfers between devices with their start and end apart: 3 -> 0, of which waited for: 1 -> 0; matrix products, arithmetic and copies ran while one was open for 3% -> 0% of each run, Pallas kernels for 0% -> 0%
where the time goes in v1:
time: 66.3 us; the launch traced here: 66 us
  Pallas kernels  56.2 us (85%)
  local copies, waits for them, and re-layouts  6.05 us (9%)
  between operations  3.7 us (6%)
    pallas_call x1, Pallas kernels, local(): pl.pallas_call(functools.partial(kernel, n_seg, n_exp, experts, gx, gc),...  56.2 us
    unnamed x4, local copies, waits for them, and re-layouts  6.05 us

profile of v1, /device:TPU:0, one launch (start us, length us, event | category | flops | bytes accessed | tf_op | source)
XLA Modules:
  0.0 66.0 jit_solution(3841645105461806231)
XLA Ops:
  1.9 1.4 %copy.14.routes = s32[1,32,2]{2,1,0:T(8,128)} copy(s32[1,32,2]{1,2,0:T(2,128)} %param.16) | data formatting | bytes 512 | tf_op args[4]
  3.3 1.4 %copy.15.norm_gain = f32[1,3,2048]{2,1,0:T(4,128)} copy(f32[1,3,2048]{2,0,1:T(1,128)} %param.17) | data formatting | bytes 49152 | tf_op args[5]
  4.6 1.8 %copy.16.router = bf16[1,2048,4]{2,1,0:T(8,128)(2,1)} copy(bf16[1,2048,4]{1,2,0:T(4,128)(2,1)} %param.18) | data formatting | bytes 32768 | tf_op args[6]
  6.4 56.2 %shard_map.131 = (bf16[1,32,2048]{2,1,0:T(8,128)(2,1)}, f32[1,1]{1,0:T(1,128)}) custom-call(bf16[1,32,2048]{2,1,0:T(8,128)(2,1)} %hidden.1, bf16[1,32,2048]{2,1,0:T(8,128)(2,1)} %memory.1, s32[1,1]{1,0:T(1,128)S(6)} %copy.19.lengths, s32[1,1]{1,0:T(1,128)S(6)} %copy.20.memory_lengths, s32[1,32,2]{2,1,0:T(8,128)} %copy.14.routes, ...), custom_call_target="tpu_custom_call" | custom-call | tf_op jit(solution)/shard_map/pallas_call | solution.py:443
  62.6 1.6 %copy.21 = bf16[1,32,2048]{2,1,0:T(8,128)(2,1)} copy(bf16[1,32,2048]{2,1,0:T(8,128)(2,1)} %get-tuple-element.8) | data formatting | bytes 262144

commit v2 on v1

--- a/solution.py
+++ b/solution.py
@@ -33,14 +33,15 @@
 
 def kernel(
     n_seg, n_exp, experts, gx, gc,
-    hidden, memory, lengths, memory_lengths, routes, norm_gain, router,
-    w_in, w_out, shortlist, student, targets,
+    hidden_any, memory, lengths, memory_lengths, routes_any, gain_any, router_any,
+    w_in, w_out, shortlist, student_any, targets,
     layer_out, loss_out,
+    hidden, routes, norm_gain, router, student, out_stage,
     win, wout, short, kmem, klen_src, klen, mid,
     out_a, out_b, x, x_b, stage, act, y0,
     core_a, core_b, rc_a, rc_b, xs_a, xs_b, rx_a, rx_b, zs_a, zs_b, z_a, z_b, z_all, z_stage,
-    lsend, lrecv, gsend, grecv,
-    wsem, msem, ra, rb, sz, sx, sc, rc_s, rc_r, rx_s, rx_r, rz_s, rz_r, l_s, l_r, g_s, g_r,
+    lsend, lrecv,
+    wsem, msem, ra, sz, sx, sc, rc_s, rc_r, rx_s, rx_r, rz_s, rz_r, l_s, l_r,
 ):
     seg = lax.axis_index("segment")
     me = lax.axis_index("expert")
@@ -58,9 +59,29 @@
     rest = cap - main
     hop_order = [k for k in range(experts // 2, experts)] + [k for k in range(1, experts // 2)]
 
+    def peer(ds, d):
+        return (lax.rem(seg + ds, n_seg), lax.rem(me + d, n_exp))
+
     def dev(e2, x2, c2):
         return (seg, (e2 * gx + x2) * gc + c2)
 
+    barrier = pltpu.get_barrier_semaphore()
+    for ds in range(n_seg):
+        for d in range(n_exp):
+            if ds or d:
+                pl.semaphore_signal(
+                    barrier, inc=1, device_id=peer(ds, d), device_id_type=MESH
+                )
+
+    early = [
+        pltpu.make_async_copy(hidden_any, hidden, wsem.at[3]),
+        pltpu.make_async_copy(gain_any, norm_gain, wsem.at[4]),
+        pltpu.make_async_copy(routes_any, routes, wsem.at[5]),
+        pltpu.make_async_copy(router_any, router, wsem.at[6]),
+        pltpu.make_async_copy(student_any, student, wsem.at[7]),
+    ]
+    for load in early:
+        load.start()
     loads = [
         pltpu.make_async_copy(w_in.at[0], win, wsem.at[0]),
         pltpu.make_async_copy(w_out.at[0], wout, wsem.at[1]),
@@ -69,21 +90,14 @@
     for load in loads:
         load.start()
 
-    barrier = pltpu.get_barrier_semaphore()
-    for d in range(1, n_exp):
-        pl.semaphore_signal(
-            barrier, inc=1, device_id=(seg, lax.rem(me + d, n_exp)), device_id_type=MESH
-        )
-    for d in range(1, n_seg):
-        pl.semaphore_signal(
-            barrier, inc=1, device_id=(lax.rem(seg + d, n_seg), me), device_id_type=MESH
-        )
     klen_src[...] = jnp.broadcast_to(memory_lengths[0:1, 0:1], klen_src.shape)
     for q in range(1, tok // LEN):
         klen_src[q : q + 1, :] = jnp.broadcast_to(memory_lengths[0:1, q : q + 1], (1, 128))
-    gains = norm_gain[0]
+    early[0].wait()
+    early[1].wait()
+    gains = [norm_gain[i] for i in range(3)]
     states = hidden[0].astype(F32)
-    pl.semaphore_wait(barrier, n_exp - 1 + n_seg - 1)
+    pl.semaphore_wait(barrier, n_exp * n_seg - 1)
 
     is_decoder = seg >= half_seg
     to_seg = lax.rem(seg + half_seg, n_seg)
@@ -102,7 +116,7 @@
 
     @pl.when(seg >= half_seg)
     def _():
-        queries = layer_norm(states, gains[0:1]).astype(BF)
+        queries = layer_norm(states, gains[0]).astype(BF)
         len_copy.wait_recv()
         mem_copy.wait_recv()
         keys = kmem[...]
@@ -140,17 +154,26 @@
                 weights[h * tok : (h + 1) * tok], keys[:, part], preferred_element_type=F32
             )
 
-    normed = layer_norm(mid[...], gains[1:2]).astype(BF)
-
+    normed = layer_norm(mid[...], gains[1]).astype(BF)
+
+    early[2].wait()
     expert_lane = lax.broadcasted_iota(jnp.int32, (tok, experts), 1)
     pos = lax.broadcasted_iota(jnp.int32, (tok, 1), 0)
     valid = jnp.zeros((tok, 1), F32)
     for q in range(tok // LEN):
         ok = (pos >= q * LEN) & (pos < (q + 1) * LEN) & (pos - q * LEN < lengths[0:1, q : q + 1])
         valid = valid + ok.astype(F32)
-    route_pair = routes[0]
-    first_hot = (route_pair[:, 0:1] == expert_lane).astype(F32)
-    second_hot = (route_pair[:, 1:2] == expert_lane).astype(F32)
+    square = lax.broadcasted_iota(jnp.int32, (tok, tok), 0) == lax.broadcasted_iota(
+        jnp.int32, (tok, tok), 1
+    )
+
+    def column(row):
+        spread = jnp.where(square, jnp.broadcast_to(row, (tok, tok)), 0)
+        return jnp.sum(spread.astype(F32), axis=-1, keepdims=True)
+
+    expert_lane = expert_lane.astype(F32)
+    first_hot = (column(routes[0, 0:1, :]) == expert_lane).astype(F32)
+    second_hot = (column(routes[0, 1:2, :]) == expert_lane).astype(F32)
     chosen = (first_hot + second_hot) * valid
     before = (
         lax.broadcasted_iota(jnp.int32, (tok, tok), 1)
@@ -202,40 +225,59 @@
     def landed(ref, sem):
         pltpu.make_async_copy(ref, ref, sem).wait()
 
-    def forward(slot_from, slot_to, sems, base, target):
-        i, o = index_b(*slot_from), index_b(*slot_to)
-        send(x.at[rows_a(*slot_from)], x.at[rows_a(*slot_to)], sems.at[base], ra.at[o], target)
-        send(x_b.at[i], x_b.at[o], sems.at[base + 1], rb.at[o], target)
+    half_width = width // 2
+
+    def piece(slot, p):
+        if p < 2:
+            return x.at[rows_a(*slot), p * half_width : (p + 1) * half_width]
+        return x_b.at[index_b(*slot)]
+
+    def arrived(slot, p):
+        landed(piece(slot, p), ra.at[3 * index_b(*slot) + p])
+
+    def forward(slot_from, slot_to, p, sems, base, target):
+        send(
+            piece(slot_from, p), piece(slot_to, p), sems.at[3 * base + p],
+            ra.at[3 * index_b(*slot_to) + p], target,
+        )
 
     for k in hop_order:
         target = dev(xor(e, k, experts), xi, ci)
-        o = index_b(0, 0, k)
-        send(out_a.at[k], x.at[rows_a(0, 0, k)], sz.at[2 * k], ra.at[o], target)
-        send(out_b.at[k], x_b.at[o], sz.at[2 * k + 1], rb.at[o], target)
+        for p in range(3):
+            src = out_a.at[k, :, p * half_width : (p + 1) * half_width] if p < 2 else out_b.at[k]
+            send(
+                src, piece((0, 0, k), p), sz.at[3 * k + p], ra.at[3 * index_b(0, 0, k) + p], target
+            )
 
     core_dev = dev(e, xi, lax.rem(ci + 1, gc))
-    for k in [0] + hop_order:
-        if k:
-            o = index_b(0, 0, k)
-            landed(x.at[rows_a(0, 0, k)], ra.at[o])
-            landed(x_b.at[o], rb.at[o])
-        for d in range(1, gx):
-            forward(
-                (0, 0, k), (0, d, k), sx, 2 * ((d - 1) * experts + k),
-                dev(e, lax.rem(xi + d, gx), ci),
-            )
-        forward((0, 0, k), (1, 0, k), sc, 2 * k, core_dev)
-    for k in [0] + hop_order:
-        for d in range(1, gx):
-            o = index_b(0, d, k)
-            landed(x.at[rows_a(0, d, k)], ra.at[o])
-            landed(x_b.at[o], rb.at[o])
-            forward((0, d, k), (1, d, k), sc, 2 * (d * experts + k), core_dev)
-    for k in [0] + hop_order:
+
+    def from_column(k):
+        for p in range(3):
+            if k:
+                arrived((0, 0, k), p)
+            for d in range(1, gx):
+                forward(
+                    (0, 0, k), (0, d, k), p, sx, (d - 1) * experts + k,
+                    dev(e, lax.rem(xi + d, gx), ci),
+                )
+            forward((0, 0, k), (1, 0, k), p, sc, k, core_dev)
+
+    def from_chips(k):
+        for p in range(3):
+            for d in range(1, gx):
+                arrived((0, d, k), p)
+                forward((0, d, k), (1, d, k), p, sc, d * experts + k, core_dev)
+
+    order = [0] + hop_order
+    for i, k in enumerate(order):
+        from_column(k)
+        if i:
+            from_chips(order[i - 1])
+    from_chips(order[-1])
+    for k in order:
         for d in range(gx):
-            o = index_b(1, d, k)
-            landed(x.at[rows_a(1, d, k)], ra.at[o])
-            landed(x_b.at[o], rb.at[o])
+            for p in range(3):
+                arrived((1, d, k), p)
 
     blocks = gx * experts
     half_rows = blocks * cap
@@ -313,7 +355,10 @@
             z_all[0:main, :] = sum_a.astype(BF)
             z_stage[0:rest, :] = sum_b
 
-    probs = jnp.dot(normed, router[0], preferred_element_type=F32)
+    early[3].wait()
+    probs = lax.dot_general(
+        normed, router[0], (((1,), (1,)), ((), ())), preferred_element_type=F32
+    )
     probs = jnp.exp(probs - jnp.max(probs, axis=-1, keepdims=True))
     probs = probs / jnp.sum(probs, axis=-1, keepdims=True)
     prob_first = jnp.sum(probs * first_hot, axis=-1, keepdims=True)
@@ -326,16 +371,11 @@
     high = combine.astype(BF)
     low = (combine - high.astype(F32)).astype(BF)
 
+    early[4].wait()
     learner_in = student[0]
     shifted = learner_in - jnp.max(learner_in, axis=-1, keepdims=True)
     learner = shifted - jnp.log(jnp.sum(jnp.exp(shifted), axis=-1, keepdims=True))
-    square = lax.broadcasted_iota(jnp.int32, (tok, tok), 0) == lax.broadcasted_iota(
-        jnp.int32, (tok, tok), 1
-    )
-    target_col = jnp.sum(
-        jnp.where(square, jnp.broadcast_to(targets[0:1, :], (tok, tok)), 0).astype(F32),
-        axis=-1, keepdims=True,
-    )
+    target_col = column(targets[0:1, :])
     vocab = student.shape[2]
     picked = lax.broadcasted_iota(jnp.int32, (tok, vocab), 1).astype(F32) == target_col
     hit = jnp.sum(jnp.where(picked, learner, 0.0), axis=-1, keepdims=True)
@@ -352,9 +392,11 @@
         low, back, preferred_element_type=F32
     )
     out = (mid[...] + moe).astype(BF)
-    layer_out[0] = out
-
-    final = layer_norm(out.astype(F32), gains[2:3]).astype(BF)
+    out_stage[...] = out
+    out_copy = pltpu.make_async_copy(out_stage, layer_out.at[0], wsem.at[8])
+    out_copy.start()
+
+    final = layer_norm(out.astype(F32), gains[2]).astype(BF)
     logits = jnp.dot(final, short[...], preferred_element_type=F32)
     logits = logits - jnp.max(logits, axis=-1, keepdims=True)
     teacher = logits - jnp.log(jnp.sum(jnp.exp(logits), axis=-1, keepdims=True))
@@ -365,29 +407,40 @@
     spot = lax.broadcasted_iota(jnp.int32, lsend.shape, 1)
     pair = jnp.where(spot == 0, loss_sum, jnp.where(spot == 1, loss_count, 0.0))
     lsend[...] = pair
-    lrecv[me] = pair
-    for d in range(1, n_exp):
-        send(
-            lsend, lrecv.at[me], l_s.at[d], l_r.at[d], (seg, lax.rem(me + d, n_exp))
-        )
-    for d in range(1, n_exp):
-        landed(lrecv.at[lax.rem(me + n_exp - d, n_exp)], l_r.at[d])
+
+    @pl.when(is_decoder)
+    def _():
+        mine = (seg - half_seg) * n_exp
+        lrecv[mine + me] = pair
+        for ds in range(n_seg):
+            for d in range(n_exp):
+                if ds or d:
+                    pltpu.make_async_remote_copy(
+                        lsend, lrecv.at[mine + me], l_s.at[ds * n_exp + d], l_r.at[mine + d],
+                        device_id=peer(ds, d), device_id_type=MESH,
+                    ).start()
+
+    for q in range(n_seg - half_seg):
+        for d in range(n_exp):
+            source = q * n_exp + lax.rem(me + n_exp - d, n_exp)
+            if d:
+                landed(lrecv.at[source], l_r.at[q * n_exp + d])
+            else:
+                @pl.when(seg != q + half_seg)
+                def _():
+                    landed(lrecv.at[source], l_r.at[q * n_exp])
+
     total = lrecv[0]
-    for i in range(1, n_exp):
+    for i in range(1, (n_seg - half_seg) * n_exp):
         total = total + lrecv[i]
-    gsend[...] = total
-    grecv[seg] = total
-    for d in range(1, n_seg):
-        send(
-            gsend, grecv.at[seg], g_s.at[d], g_r.at[d], (lax.rem(seg + d, n_seg), me)
-        )
-    for d in range(1, n_seg):
-        landed(grecv.at[lax.rem(seg + n_seg - d, n_seg)], g_r.at[d])
-    total = grecv[0]
-    for i in range(1, n_seg):
-        total = total + grecv[i]
     loss_out[...] = total[0:1, 0:1] / total[0:1, 1:2]
 
+    @pl.when(is_decoder)
+    def _():
+        for i in range(1, n_seg * n_exp):
+            pltpu.make_async_copy(lsend, lsend, l_s.at[i]).wait()
+
+    out_copy.wait()
     for copy in waits:
         copy.wait_send()
 
@@ -421,6 +474,8 @@
     dma = pltpu.SemaphoreType.DMA
     nx = max(gx - 1, 1) * experts
     scratch = [
+        v((1, tok, width), BF), v((1, 2, tok), jnp.int32), v((3, 1, width), F32),
+        v((1, experts, width), BF), v((1, tok, vocab), F32), v((tok, width), BF),
         v((width, units), BF), v((units, width), BF), v((width, vocab), BF),
         v((tok, width), BF), v((8, 128), jnp.int32), v((8, 128), jnp.int32), v((tok, width), F32),
         v((experts, main, width), BF), v((experts, rest, width), BF),
@@ -433,12 +488,12 @@
         v((experts, main, width), BF), v((experts, rest, width), BF),
         v((experts, main, width), BF), v((experts, rest, width), BF),
         v((experts * cap, width), BF), v((experts * rest, width), F32),
-        v((8, 128), F32), v((n_exp, 8, 128), F32), v((8, 128), F32), v((n_seg, 8, 128), F32),
-        dma((3,)), dma((4,)), dma((gc * blocks,)), dma((gc * blocks,)),
-        dma((2 * experts,)), dma((2 * nx,)), dma((2 * blocks,)),
+        v((8, 128), F32), v(((n_seg - n_seg // 2) * n_exp, 8, 128), F32),
+        dma((9,)), dma((4,)), dma((3 * gc * blocks,)),
+        dma((3 * experts,)), dma((3 * nx,)), dma((3 * blocks,)),
         dma((2,)), dma((2,)), dma((2 * nx,)), dma((2 * nx,)),
         dma((2 * experts,)), dma((2 * experts,)),
-        dma((n_exp,)), dma((n_exp,)), dma((n_seg,)), dma((n_seg,)),
+        dma((n_seg * n_exp,)), dma(((n_seg - n_seg // 2) * n_exp,)),
     ]
     layer_out, loss = pl.pallas_call(
         functools.partial(kernel, n_seg, n_exp, experts, gx, gc),
@@ -446,14 +501,15 @@
             jax.ShapeDtypeStruct((1, tok, width), BF),
             jax.ShapeDtypeStruct((1, 1), F32),
         ),
-        in_specs=[vm, hbm, vm, vm, vm, vm, vm, hbm, hbm, hbm, vm, vm],
-        out_specs=(vm, vm),
+        in_specs=[hbm, hbm, vm, vm, hbm, hbm, hbm, hbm, hbm, hbm, hbm, vm],
+        out_specs=(hbm, vm),
         scratch_shapes=scratch,
         compiler_params=pltpu.CompilerParams(
             collective_id=0, has_side_effects=True, vmem_limit_bytes=60 * 1024 * 1024
         ),
     )(
-        hidden, memory, lengths, memory_lengths, routes, norm_gain, router,
+        hidden, memory, lengths, memory_lengths, jnp.swapaxes(routes, 1, 2),
+        jnp.swapaxes(norm_gain, 0, 1), jnp.swapaxes(router, 1, 2),
         w_in, w_out, shortlist, student, targets,
     )
     return layer_out, loss[0, 0]

time: 66.3 us -> 61 us (0.920)
  local copies, waits for them, and re-layouts: 6.05 us -> 1.57 us
  Pallas kernels: 56.2 us -> 55.5 us
    unnamed x4 -> x1, local copies, waits for them, and re-layouts: 6.05 us -> 1.57 us
    pallas_call x1, Pallas kernels: 56.2 us -> 55.5 us  [local(): pl.pallas_call(functools.partial(kernel, n_seg, n_exp, experts, gx, gc),...]
where the time goes in v2:
time: 61 us; the launch traced here: 60.8 us
  Pallas kernels  55.5 us (91%)
  between operations  3.74 us (6%)
  local copies, waits for them, and re-layouts  1.57 us (3%)
    pallas_call x1, Pallas kernels, local(): pl.pallas_call(functools.partial(kernel, n_seg, n_exp, experts, gx, gc),...  55.5 us
    unnamed x1, local copies, waits for them, and re-layouts  1.57 us

profile of v2, /device:TPU:0, one launch (start us, length us, event | category | flops | bytes accessed | tf_op | source)
XLA Modules:
  0.0 60.8 jit_solution(9523053632223755384)
XLA Ops:
  1.9 55.5 %shard_map.131 = (bf16[1,32,2048]{2,1,0:T(8,128)(2,1)}, f32[1,1]{1,0:T(1,128)}) custom-call(bf16[1,32,2048]{2,1,0:T(8,128)(2,1)} %hidden_any.1, bf16[1,32,2048]{2,1,0:T(8,128)(2,1)} %memory.1, s32[1,1]{1,0:T(1,128)S(6)} %copy.16.lengths, s32[1,1]{1,0:T(1,128)S(6)} %copy.17.memory_lengths, s32[1,2,32]{2,1,0:T(2,128)} %bitcast.6, f32[3,1,2048]{2,1,0:T(1,128)} %bitcast.4, ...), custom_call_target="tpu_custom_call" | custom-call | tf_op jit(solution)/shard_map/pallas_call | solution.py:498
  57.4 1.6 %copy.18 = bf16[1,32,2048]{2,1,0:T(8,128)(2,1)} copy(bf16[1,32,2048]{2,1,0:T(8,128)(2,1)} %get-tuple-element.8) | data formatting | bytes 262144

commit v3 on v2

--- a/solution.py
+++ b/solution.py
@@ -57,7 +57,12 @@
     cap = 5 * tok // 8
     main = cap // 16 * 16
     rest = cap - main
-    hop_order = [k for k in range(experts // 2, experts)] + [k for k in range(1, experts // 2)]
+    hop_order = list(range(experts - 1, 0, -1))
+    back_order = hop_order + [0]
+    span = experts // 2
+    turns = [back_order[0:span], back_order[span:]]
+    chunk_main = gx * span * main
+    chunk = gx * span * cap
 
     def peer(ds, d):
         return (lax.rem(seg + ds, n_seg), lax.rem(me + d, n_exp))
@@ -101,25 +106,32 @@
 
     is_decoder = seg >= half_seg
     to_seg = lax.rem(seg + half_seg, n_seg)
-    mem_copy = pltpu.make_async_remote_copy(
-        memory.at[0], kmem, msem.at[0], msem.at[1], device_id=(to_seg, me), device_id_type=MESH
-    )
+    mem_parts = 4 if heads % 4 == 0 else 1
+    mem_width = width // mem_parts
+    mem_copies = []
+    for p in range(mem_parts):
+        part = slice(p * mem_width, (p + 1) * mem_width)
+        mem_copies.append(
+            pltpu.make_async_remote_copy(
+                memory.at[0, :, part], kmem.at[:, part], msem.at[2 + p], msem.at[6 + p],
+                device_id=(to_seg, me), device_id_type=MESH,
+            )
+        )
     len_copy = pltpu.make_async_remote_copy(
-        klen_src, klen, msem.at[2], msem.at[3], device_id=(to_seg, me), device_id_type=MESH
+        klen_src, klen, msem.at[0], msem.at[1], device_id=(to_seg, me), device_id_type=MESH
     )
 
     @pl.when(seg < half_seg)
     def _():
-        mem_copy.start()
         len_copy.start()
+        for copy in mem_copies:
+            copy.start()
         mid[...] = states
 
     @pl.when(seg >= half_seg)
     def _():
         queries = layer_norm(states, gains[0]).astype(BF)
         len_copy.wait_recv()
-        mem_copy.wait_recv()
-        keys = kmem[...]
         col = lax.broadcasted_iota(jnp.int32, (tok, tok), 1)
         row = lax.broadcasted_iota(jnp.int32, (tok, tok), 0)
         klen_v = klen[...]
@@ -128,31 +140,32 @@
             inside = (col >= q * LEN) & (col - q * LEN < klen_v[q : q + 1, 0:1])
             inside = inside & (col < (q + 1) * LEN) & (row >= q * LEN) & (row < (q + 1) * LEN)
             allowed = allowed | inside
-        scores = jnp.concatenate(
-            [
-                jnp.where(
-                    allowed,
-                    lax.dot_general(
-                        queries[:, h * HEAD_DIM : (h + 1) * HEAD_DIM],
-                        keys[:, h * HEAD_DIM : (h + 1) * HEAD_DIM],
-                        (((1,), (1,)), ((), ())),
-                        preferred_element_type=F32,
+        for p in range(mem_parts):
+            mem_copies[p].wait_recv()
+            span_heads = range(p * heads // mem_parts, (p + 1) * heads // mem_parts)
+            parts = [slice(h * HEAD_DIM, (h + 1) * HEAD_DIM) for h in span_heads]
+            scores = jnp.concatenate(
+                [
+                    jnp.where(
+                        allowed,
+                        lax.dot_general(
+                            queries[:, part], kmem[:, part], (((1,), (1,)), ((), ())),
+                            preferred_element_type=F32,
+                        )
+                        * (1.0 / math.sqrt(HEAD_DIM)),
+                        -1e30,
                     )
-                    * (1.0 / math.sqrt(HEAD_DIM)),
-                    -1e30,
+                    for part in parts
+                ],
+                axis=0,
+            )
+            top = jnp.max(scores, axis=-1, keepdims=True)
+            raised = jnp.exp(scores - top)
+            weights = (raised / jnp.sum(raised, axis=-1, keepdims=True)).astype(BF)
+            for i, part in enumerate(parts):
+                mid[:, part] = states[:, part] + jnp.dot(
+                    weights[i * tok : (i + 1) * tok], kmem[:, part], preferred_element_type=F32
                 )
-                for h in range(heads)
-            ],
-            axis=0,
-        )
-        top = jnp.max(scores, axis=-1, keepdims=True)
-        raised = jnp.exp(scores - top)
-        weights = (raised / jnp.sum(raised, axis=-1, keepdims=True)).astype(BF)
-        for h in range(heads):
-            part = slice(h * HEAD_DIM, (h + 1) * HEAD_DIM)
-            mid[:, part] = states[:, part] + jnp.dot(
-                weights[h * tok : (h + 1) * tok], keys[:, part], preferred_element_type=F32
-            )
 
     normed = layer_norm(mid[...], gains[1]).astype(BF)
 
@@ -201,8 +214,13 @@
     place_rows = jnp.transpose(placing)[0:n_slots].astype(BF)
     slots = jnp.dot(place_rows, normed, preferred_element_type=F32)
 
+    def place(dc, dx, k):
+        turn = 0 if k in turns[0] else 1
+        return turn, turn * gc + gc - 1 - dc, dx * span + turns[turn].index(k)
+
     def rows_a(dc, dx, k):
-        return pl.ds(dc * gx * experts * cap + (dx * experts + k) * main, main)
+        _, part, b = place(dc, dx, k)
+        return pl.ds(part * chunk + b * main, main)
 
     def index_b(dc, dx, k):
         return (dc * gx + dx) * experts + k
@@ -280,12 +298,13 @@
                 arrived((1, d, k), p)
 
     blocks = gx * experts
-    half_rows = blocks * cap
-    half_main = blocks * main
     for dc in range(gc):
-        for i in range(blocks):
-            stage[i * rest : (i + 1) * rest, :] = x_b[dc * blocks + i].astype(F32)
-        x[dc * half_rows + half_main : (dc + 1) * half_rows, :] = stage[...].astype(BF)
+        for turn in range(2):
+            for dx in range(gx):
+                for k in turns[turn]:
+                    _, part, b = place(dc, dx, k)
+                    stage[b * rest : (b + 1) * rest, :] = x_b[index_b(dc, dx, k)].astype(F32)
+            x[part * chunk + chunk_main : (part + 1) * chunk, :] = stage[...].astype(BF)
 
     units = win.shape[1]
     tile = min(256, units)
@@ -301,42 +320,50 @@
     loads[1].wait()
     tile2 = 256
 
-    @pl.loop(0, width // tile2)
-    def _(i):
-        cols = pl.ds(pl.multiple_of(i * tile2, tile2), tile2)
-        part = jnp.dot(act[half_rows:, :], wout[:, cols], preferred_element_type=F32)
-        core_a[:, cols] = part[0:half_main].astype(BF)
-        for b in range(blocks):
-            core_b[b, :, cols] = part[half_main + b * rest : half_main + (b + 1) * rest].astype(BF)
-
-    send(core_a, rc_a, rc_s.at[0], rc_r.at[0], core_dev)
-    send(core_b, rc_b, rc_s.at[1], rc_r.at[1], core_dev)
-
-    @pl.loop(0, width // tile2)
-    def _(i):
-        cols = pl.ds(pl.multiple_of(i * tile2, tile2), tile2)
-        y0[:, cols] = jnp.dot(act[0:half_rows, :], wout[:, cols], preferred_element_type=F32)
-
-    landed(rc_a, rc_r.at[0])
-    landed(rc_b, rc_r.at[1])
-
     def chip_sum(dx, k):
-        b = dx * experts + k
-        sum_a = y0[b * main : (b + 1) * main, :] + rc_a[b * main : (b + 1) * main, :].astype(F32)
-        low = half_main + b * rest
-        sum_b = y0[low : low + rest, :] + rc_b[b].astype(F32)
+        turn, _, b = place(0, dx, k)
+        top = turn * chunk + b * main
+        sum_a = y0[top : top + main, :] + rc_a[turn, b * main : (b + 1) * main, :].astype(F32)
+        low = turn * chunk + chunk_main + b * rest
+        sum_b = y0[low : low + rest, :] + rc_b[turn, b].astype(F32)
         return sum_a, sum_b
 
-    back_order = hop_order + [0]
-    for k in back_order:
-        for d in range(1, gx):
-            o = (d - 1) * experts + k
-            sum_a, sum_b = chip_sum(d, k)
-            xs_a[o] = sum_a.astype(BF)
-            xs_b[o] = sum_b.astype(BF)
-            target = dev(e, lax.rem(xi + gx - d, gx), ci)
-            send(xs_a.at[o], rx_a.at[o], rx_s.at[2 * o], rx_r.at[2 * o], target)
-            send(xs_b.at[o], rx_b.at[o], rx_s.at[2 * o + 1], rx_r.at[2 * o + 1], target)
+    def second(turn):
+        @pl.loop(0, width // tile2)
+        def _(i):
+            cols = pl.ds(pl.multiple_of(i * tile2, tile2), tile2)
+            rows = act[turn * gc * chunk : (turn * gc + 1) * chunk, :]
+            part = jnp.dot(rows, wout[:, cols], preferred_element_type=F32)
+            core_a[turn, :, cols] = part[0:chunk_main].astype(BF)
+            for b in range(gx * span):
+                low = chunk_main + b * rest
+                core_b[turn, b, :, cols] = part[low : low + rest].astype(BF)
+
+        send(core_a.at[turn], rc_a.at[turn], rc_s.at[2 * turn], rc_r.at[2 * turn], core_dev)
+        send(core_b.at[turn], rc_b.at[turn], rc_s.at[2 * turn + 1], rc_r.at[2 * turn + 1], core_dev)
+
+        @pl.loop(0, width // tile2)
+        def _(i):
+            cols = pl.ds(pl.multiple_of(i * tile2, tile2), tile2)
+            rows = act[(turn * gc + 1) * chunk : (turn + 1) * gc * chunk, :]
+            y0[turn * chunk : (turn + 1) * chunk, cols] = jnp.dot(
+                rows, wout[:, cols], preferred_element_type=F32
+            )
+
+        landed(rc_a.at[turn], rc_r.at[2 * turn])
+        landed(rc_b.at[turn], rc_r.at[2 * turn + 1])
+        for k in turns[turn]:
+            for d in range(1, gx):
+                o = (d - 1) * experts + k
+                sum_a, sum_b = chip_sum(d, k)
+                xs_a[o] = sum_a.astype(BF)
+                xs_b[o] = sum_b.astype(BF)
+                target = dev(e, lax.rem(xi + gx - d, gx), ci)
+                send(xs_a.at[o], rx_a.at[o], rx_s.at[2 * o], rx_r.at[2 * o], target)
+                send(xs_b.at[o], rx_b.at[o], rx_s.at[2 * o + 1], rx_r.at[2 * o + 1], target)
+
+    second(0)
+    second(1)
     for k in back_order:
         sum_a, sum_b = chip_sum(0, k)
         for d in range(1, gx):
@@ -446,8 +473,9 @@
 
     @pl.when(seg < half_seg)
     def _():
-        mem_copy.wait_send()
         len_copy.wait_send()
+        for copy in mem_copies:
+            copy.wait_send()
 
 
 def local(
@@ -468,6 +496,7 @@
     rest = cap - main
     blocks = gx * experts
     half_rows = blocks * cap
+    span = experts // 2
     vm = pl.BlockSpec(memory_space=pltpu.VMEM)
     hbm = pl.BlockSpec(memory_space=pl.ANY)
     v = pltpu.VMEM
@@ -480,18 +509,18 @@
         v((tok, width), BF), v((8, 128), jnp.int32), v((8, 128), jnp.int32), v((tok, width), F32),
         v((experts, main, width), BF), v((experts, rest, width), BF),
         v((gc * half_rows, width), BF), v((gc * blocks, rest, width), BF),
-        v((blocks * rest, width), F32), v((gc * half_rows, units), BF), v((half_rows, width), F32),
-        v((blocks * main, width), BF), v((blocks, rest, width), BF),
-        v((blocks * main, width), BF), v((blocks, rest, width), BF),
+        v((gx * span * rest, width), F32), v((gc * half_rows, units), BF), v((half_rows, width), F32),
+        v((2, gx * span * main, width), BF), v((2, gx * span, rest, width), BF),
+        v((2, gx * span * main, width), BF), v((2, gx * span, rest, width), BF),
         v((nx, main, width), BF), v((nx, rest, width), BF),
         v((nx, main, width), BF), v((nx, rest, width), BF),
         v((experts, main, width), BF), v((experts, rest, width), BF),
         v((experts, main, width), BF), v((experts, rest, width), BF),
         v((experts * cap, width), BF), v((experts * rest, width), F32),
-        v((8, 128), F32), v(((n_seg - n_seg // 2) * n_exp, 8, 128), F32),
-        dma((9,)), dma((4,)), dma((3 * gc * blocks,)),
+        v((1, 128), F32), v(((n_seg - n_seg // 2) * n_exp, 1, 128), F32),
+        dma((9,)), dma((10,)), dma((3 * gc * blocks,)),
         dma((3 * experts,)), dma((3 * nx,)), dma((3 * blocks,)),
-        dma((2,)), dma((2,)), dma((2 * nx,)), dma((2 * nx,)),
+        dma((4,)), dma((4,)), dma((2 * nx,)), dma((2 * nx,)),
         dma((2 * experts,)), dma((2 * experts,)),
         dma((n_seg * n_exp,)), dma(((n_seg - n_seg // 2) * n_exp,)),
     ]

time: 61 us -> 61.2 us (level)
  no operation moved by 1% of the time
where the time goes in v3:
time: 61.2 us; the launch traced here: 61 us
  Pallas kernels  55.7 us (91%)
  between operations  3.74 us (6%)
  local copies, waits for them, and re-layouts  1.57 us (3%)
    pallas_call x1, Pallas kernels, local(): pl.pallas_call(functools.partial(kernel, n_seg, n_exp, experts, gx, gc),...  55.7 us
    unnamed x1, local copies, waits for them, and re-layouts  1.57 us

profile of v3, /device:TPU:0, one launch (start us, length us, event | category | flops | bytes accessed | tf_op | source)
XLA Modules:
  0.0 61.0 jit_solution(9938646286513826488)
XLA Ops:
  1.9 55.7 %shard_map.131 = (bf16[1,32,2048]{2,1,0:T(8,128)(2,1)}, f32[1,1]{1,0:T(1,128)}) custom-call(bf16[1,32,2048]{2,1,0:T(8,128)(2,1)} %hidden_any.1, bf16[1,32,2048]{2,1,0:T(8,128)(2,1)} %memory.1, s32[1,1]{1,0:T(1,128)S(6)} %copy.16.lengths, s32[1,1]{1,0:T(1,128)S(6)} %copy.17.memory_lengths, s32[1,2,32]{2,1,0:T(2,128)} %bitcast.6, f32[3,1,2048]{2,1,0:T(1,128)} %bitcast.4, ...), custom_call_target="tpu_custom_call" | custom-call | tf_op jit(solution)/shard_map/pallas_call | solution.py:527
  57.6 1.6 %copy.18 = bf16[1,32,2048]{2,1,0:T(8,128)(2,1)} copy(bf16[1,32,2048]{2,1,0:T(8,128)(2,1)} %get-tuple-element.8) | data formatting | bytes 262144

commit v4 on v3

--- a/solution.py
+++ b/solution.py
@@ -40,7 +40,7 @@
     win, wout, short, kmem, klen_src, klen, mid,
     out_a, out_b, x, x_b, stage, act, y0,
     core_a, core_b, rc_a, rc_b, xs_a, xs_b, rx_a, rx_b, zs_a, zs_b, z_a, z_b, z_all, z_stage,
-    lsend, lrecv,
+    lsend, l_plane, l_hop, l_seg,
     wsem, msem, ra, sz, sx, sc, rc_s, rc_r, rx_s, rx_r, rz_s, rz_r, l_s, l_r,
 ):
     seg = lax.axis_index("segment")
@@ -59,24 +59,29 @@
     rest = cap - main
     hop_order = list(range(experts - 1, 0, -1))
     back_order = hop_order + [0]
-    span = experts // 2
-    turns = [back_order[0:span], back_order[span:]]
+    span = experts
+    turns = [back_order]
     chunk_main = gx * span * main
     chunk = gx * span * cap
 
-    def peer(ds, d):
-        return (lax.rem(seg + ds, n_seg), lax.rem(me + d, n_exp))
-
     def dev(e2, x2, c2):
         return (seg, (e2 * gx + x2) * gc + c2)
 
     barrier = pltpu.get_barrier_semaphore()
-    for ds in range(n_seg):
-        for d in range(n_exp):
-            if ds or d:
-                pl.semaphore_signal(
-                    barrier, inc=1, device_id=peer(ds, d), device_id_type=MESH
-                )
+    def plane_peer(d):
+        return (seg, e * group + lax.rem(j + d, group))
+
+    def hop_peer(k):
+        return (seg, xor(e, k, experts) * group + j)
+
+    def seg_peer(d):
+        return (lax.rem(seg + d, n_seg), me)
+
+    partners = [plane_peer(d) for d in range(1, group)]
+    partners += [hop_peer(k) for k in range(1, experts)]
+    partners += [seg_peer(d) for d in range(1, n_seg)]
+    for target in partners:
+        pl.semaphore_signal(barrier, inc=1, device_id=target, device_id_type=MESH)
 
     early = [
         pltpu.make_async_copy(hidden_any, hidden, wsem.at[3]),
@@ -102,7 +107,7 @@
     early[1].wait()
     gains = [norm_gain[i] for i in range(3)]
     states = hidden[0].astype(F32)
-    pl.semaphore_wait(barrier, n_exp * n_seg - 1)
+    pl.semaphore_wait(barrier, len(partners))
 
     is_decoder = seg >= half_seg
     to_seg = lax.rem(seg + half_seg, n_seg)
@@ -299,7 +304,7 @@
 
     blocks = gx * experts
     for dc in range(gc):
-        for turn in range(2):
+        for turn in range(len(turns)):
             for dx in range(gx):
                 for k in turns[turn]:
                     _, part, b = place(dc, dx, k)
@@ -363,7 +368,6 @@
                 send(xs_b.at[o], rx_b.at[o], rx_s.at[2 * o + 1], rx_r.at[2 * o + 1], target)
 
     second(0)
-    second(1)
     for k in back_order:
         sum_a, sum_b = chip_sum(0, k)
         for d in range(1, gx):
@@ -431,42 +435,34 @@
     counted = jnp.where(is_decoder, valid, 0.0)
     loss_sum = jnp.sum(token_loss * counted, axis=0, keepdims=True)
     loss_count = jnp.sum(counted, axis=0, keepdims=True)
-    spot = lax.broadcasted_iota(jnp.int32, lsend.shape, 1)
+    spot = lax.broadcasted_iota(jnp.int32, (1, 128), 1)
     pair = jnp.where(spot == 0, loss_sum, jnp.where(spot == 1, loss_count, 0.0))
-    lsend[...] = pair
-
-    @pl.when(is_decoder)
-    def _():
-        mine = (seg - half_seg) * n_exp
-        lrecv[mine + me] = pair
-        for ds in range(n_seg):
-            for d in range(n_exp):
-                if ds or d:
-                    pltpu.make_async_remote_copy(
-                        lsend, lrecv.at[mine + me], l_s.at[ds * n_exp + d], l_r.at[mine + d],
-                        device_id=peer(ds, d), device_id_type=MESH,
-                    ).start()
-
-    for q in range(n_seg - half_seg):
-        for d in range(n_exp):
-            source = q * n_exp + lax.rem(me + n_exp - d, n_exp)
-            if d:
-                landed(lrecv.at[source], l_r.at[q * n_exp + d])
-            else:
-                @pl.when(seg != q + half_seg)
-                def _():
-                    landed(lrecv.at[source], l_r.at[q * n_exp])
-
-    total = lrecv[0]
-    for i in range(1, (n_seg - half_seg) * n_exp):
-        total = total + lrecv[i]
+
+    def added(value, out_row, table, here, count, peers, arrivals, base):
+        out_row[...] = value
+        table[here] = value
+        for i, target in enumerate(peers):
+            send(out_row, table.at[here], l_s.at[base + i], l_r.at[base + i], target)
+        for i, source in enumerate(arrivals):
+            landed(table.at[source], l_r.at[base + i])
+        result = table[0]
+        for i in range(1, count):
+            result = result + table[i]
+        return result
+
+    total = added(
+        pair, lsend.at[0], l_plane, j, group, partners[0 : group - 1],
+        [lax.rem(j + group - d, group) for d in range(1, group)], 0,
+    )
+    total = added(
+        total, lsend.at[1], l_hop, e, experts, partners[group - 1 : group + experts - 2],
+        [xor(e, k, experts) for k in range(1, experts)], group - 1,
+    )
+    total = added(
+        total, lsend.at[2], l_seg, seg, n_seg, partners[group + experts - 2 :],
+        [lax.rem(seg + n_seg - d, n_seg) for d in range(1, n_seg)], group + experts - 2,
+    )
     loss_out[...] = total[0:1, 0:1] / total[0:1, 1:2]
-
-    @pl.when(is_decoder)
-    def _():
-        for i in range(1, n_seg * n_exp):
-            pltpu.make_async_copy(lsend, lsend, l_s.at[i]).wait()
-
     out_copy.wait()
     for copy in waits:
         copy.wait_send()
@@ -496,7 +492,7 @@
     rest = cap - main
     blocks = gx * experts
     half_rows = blocks * cap
-    span = experts // 2
+    span = experts
     vm = pl.BlockSpec(memory_space=pltpu.VMEM)
     hbm = pl.BlockSpec(memory_space=pl.ANY)
     v = pltpu.VMEM
@@ -510,19 +506,19 @@
         v((experts, main, width), BF), v((experts, rest, width), BF),
         v((gc * half_rows, width), BF), v((gc * blocks, rest, width), BF),
         v((gx * span * rest, width), F32), v((gc * half_rows, units), BF), v((half_rows, width), F32),
-        v((2, gx * span * main, width), BF), v((2, gx * span, rest, width), BF),
-        v((2, gx * span * main, width), BF), v((2, gx * span, rest, width), BF),
+        v((1, gx * span * main, width), BF), v((1, gx * span, rest, width), BF),
+        v((1, gx * span * main, width), BF), v((1, gx * span, rest, width), BF),
         v((nx, main, width), BF), v((nx, rest, width), BF),
         v((nx, main, width), BF), v((nx, rest, width), BF),
         v((experts, main, width), BF), v((experts, rest, width), BF),
         v((experts, main, width), BF), v((experts, rest, width), BF),
         v((experts * cap, width), BF), v((experts * rest, width), F32),
-        v((1, 128), F32), v(((n_seg - n_seg // 2) * n_exp, 1, 128), F32),
+        v((3, 1, 128), F32), v((group, 1, 128), F32), v((experts, 1, 128), F32), v((n_seg, 1, 128), F32),
         dma((9,)), dma((10,)), dma((3 * gc * blocks,)),
         dma((3 * experts,)), dma((3 * nx,)), dma((3 * blocks,)),
         dma((4,)), dma((4,)), dma((2 * nx,)), dma((2 * nx,)),
         dma((2 * experts,)), dma((2 * experts,)),
-        dma((n_seg * n_exp,)), dma(((n_seg - n_seg // 2) * n_exp,)),
+        dma((group + experts + n_seg,)), dma((group + experts + n_seg,)),
     ]
     layer_out, loss = pl.pallas_call(
         functools.partial(kernel, n_seg, n_exp, experts, gx, gc),

time: 61.2 us -> 62.2 us (1.016)
  Pallas kernels: 55.7 us -> 56.7 us
    pallas_call x1, Pallas kernels: 55.7 us -> 56.7 us  [local(): pl.pallas_call(functools.partial(kernel, n_seg, n_exp, experts, gx, gc),...]
where the time goes in v4:
time: 62.2 us; the launch traced here: 62 us
  Pallas kernels  56.7 us (91%)
  between operations  3.74 us (6%)
  local copies, waits for them, and re-layouts  1.57 us (3%)
    pallas_call x1, Pallas kernels, local(): pl.pallas_call(functools.partial(kernel, n_seg, n_exp, experts, gx, gc),...  56.7 us
    unnamed x1, local copies, waits for them, and re-layouts  1.57 us

profile of v4, /device:TPU:0, one launch (start us, length us, event | category | flops | bytes accessed | tf_op | source)
XLA Modules:
  0.0 62.0 jit_solution(13588048572956724589)
XLA Ops:
  1.9 56.7 %shard_map.131 = (bf16[1,32,2048]{2,1,0:T(8,128)(2,1)}, f32[1,1]{1,0:T(1,128)}) custom-call(bf16[1,32,2048]{2,1,0:T(8,128)(2,1)} %hidden_any.1, bf16[1,32,2048]{2,1,0:T(8,128)(2,1)} %memory.1, s32[1,1]{1,0:T(1,128)S(6)} %copy.16.lengths, s32[1,1]{1,0:T(1,128)S(6)} %copy.17.memory_lengths, s32[1,2,32]{2,1,0:T(2,128)} %bitcast.6, f32[3,1,2048]{2,1,0:T(1,128)} %bitcast.4, ...), custom_call_target="tpu_custom_call" | custom-call | tf_op jit(solution)/shard_map/pallas_call | solution.py:523
  58.7 1.6 %copy.18 = bf16[1,32,2048]{2,1,0:T(8,128)(2,1)} copy(bf16[1,32,2048]{2,1,0:T(8,128)(2,1)} %get-tuple-element.8) | data formatting | bytes 262144

commit v5 on v3

--- a/solution.py
+++ b/solution.py
@@ -59,8 +59,8 @@
     rest = cap - main
     hop_order = list(range(experts - 1, 0, -1))
     back_order = hop_order + [0]
-    span = experts // 2
-    turns = [back_order[0:span], back_order[span:]]
+    span = experts
+    turns = [back_order]
     chunk_main = gx * span * main
     chunk = gx * span * cap
 
@@ -299,7 +299,7 @@
 
     blocks = gx * experts
     for dc in range(gc):
-        for turn in range(2):
+        for turn in range(len(turns)):
             for dx in range(gx):
                 for k in turns[turn]:
                     _, part, b = place(dc, dx, k)
@@ -363,7 +363,6 @@
                 send(xs_b.at[o], rx_b.at[o], rx_s.at[2 * o + 1], rx_r.at[2 * o + 1], target)
 
     second(0)
-    second(1)
     for k in back_order:
         sum_a, sum_b = chip_sum(0, k)
         for d in range(1, gx):
@@ -496,7 +495,7 @@
     rest = cap - main
     blocks = gx * experts
     half_rows = blocks * cap
-    span = experts // 2
+    span = experts
     vm = pl.BlockSpec(memory_space=pltpu.VMEM)
     hbm = pl.BlockSpec(memory_space=pl.ANY)
     v = pltpu.VMEM
@@ -510,8 +509,8 @@
         v((experts, main, width), BF), v((experts, rest, width), BF),
         v((gc * half_rows, width), BF), v((gc * blocks, rest, width), BF),
         v((gx * span * rest, width), F32), v((gc * half_rows, units), BF), v((half_rows, width), F32),
-        v((2, gx * span * main, width), BF), v((2, gx * span, rest, width), BF),
-        v((2, gx * span * main, width), BF), v((2, gx * span, rest, width), BF),
+        v((1, gx * span * main, width), BF), v((1, gx * span, rest, width), BF),
+        v((1, gx * span * main, width), BF), v((1, gx * span, rest, width), BF),
         v((nx, main, width), BF), v((nx, rest, width), BF),
         v((nx, main, width), BF), v((nx, rest, width), BF),
         v((experts, main, width), BF), v((experts, rest, width), BF),

time: 61.2 us -> 61.4 us (level)
  no operation moved by 1% of the time
where the time goes in v5:
time: 61.4 us; the launch traced here: 61.2 us
  Pallas kernels  55.9 us (91%)
  between operations  3.74 us (6%)
  local copies, waits for them, and re-layouts  1.57 us (3%)
    pallas_call x1, Pallas kernels, local(): pl.pallas_call(functools.partial(kernel, n_seg, n_exp, experts, gx, gc),...  55.9 us
    unnamed x1, local copies, waits for them, and re-layouts  1.57 us

profile of v5, /device:TPU:0, one launch (start us, length us, event | category | flops | bytes accessed | tf_op | source)
XLA Modules:
  0.0 61.2 jit_solution(11115715638705687972)
XLA Ops:
  1.9 55.9 %shard_map.131 = (bf16[1,32,2048]{2,1,0:T(8,128)(2,1)}, f32[1,1]{1,0:T(1,128)}) custom-call(bf16[1,32,2048]{2,1,0:T(8,128)(2,1)} %hidden_any.1, bf16[1,32,2048]{2,1,0:T(8,128)(2,1)} %memory.1, s32[1,1]{1,0:T(1,128)S(6)} %copy.16.lengths, s32[1,1]{1,0:T(1,128)S(6)} %copy.17.memory_lengths, s32[1,2,32]{2,1,0:T(2,128)} %bitcast.6, f32[3,1,2048]{2,1,0:T(1,128)} %bitcast.4, ...), custom_call_target="tpu_custom_call" | custom-call | tf_op jit(solution)/shard_map/pallas_call | solution.py:526
  57.8 1.6 %copy.18 = bf16[1,32,2048]{2,1,0:T(8,128)(2,1)} copy(bf16[1,32,2048]{2,1,0:T(8,128)(2,1)} %get-tuple-element.8) | data formatting | bytes 262144
